TPU v7x, 32 devices: a whole 2x2x4 slice. The times are simulated.
32 devices in a mesh: section: 2 (over x), head: 4 (over y, core), dp: 4 (over z).
Axes of the slice: x: 2, y: 2, z: 4, core: 2. Of those that a mesh axis runs over, the one named last changes fastest.
Arguments:
- tokens: bfloat16 [4, 2, 1536, 768], P('dp', None, 'head'), may hold values from -6 to 6
- images: int32 [4, 2, 1536], P('dp'), may hold values from 0 to 5, never falling along the last dimension, each value on 1 to 1024 neighbouring positions
- norm_gain: float32 [2, 2, 768], P('section'), may hold values from 0.5 to 1.5
- norm_shift: float32 [2, 2, 768], P('section'), may hold values from -1.5 to 1.5
- input_bias: float32 [2, 2, 768], P('section', None, 'head'), may hold values from -2.5 to 2.5
- project_in: bfloat16 [2, 3, 768, 768], P('section', None, None, 'head'), may hold values from -0.21875 to 0.21875
- project_out: bfloat16 [2, 768, 768], P('section', 'head'), may hold values from -1.75 to 1.75
- branch_bias: float32 [2, 2, 768], P('section'), may hold values from -1.5 to 1.5
- layer_scale: float32 [2, 2, 768], P('section'), may hold values from 0.5 to 2
- expand_bias: float32 [2, 3072], P('section', 'head'), may hold values from -1.5 to 1.5
- expand_weight: bfloat16 [2, 768, 3072], P('section', None, 'head'), may hold values from -0.21875 to 0.21875
- reduce_weight: bfloat16 [2, 3072, 768], P('section', 'head'), may hold values from -0.109375 to 0.109375
- cotangent: bfloat16 [4, 2, 1536, 768], P('dp', None, 'head'), may hold values from -6 to 6
Outputs:
- final_tokens: bfloat16 [4, 2, 1536, 768], P('dp', 'section', 'head')
- grad_tokens: bfloat16 [4, 2, 1536, 768], P('dp', 'section', 'head')
- grad_norm_gain: float32 [2, 2, 768], P('section')
- grad_norm_shift: float32 [2, 2, 768], P('section')
- grad_input_bias: float32 [2, 2, 768], P('section', None, 'head')
- grad_project_in: float32 [2, 3, 768, 768], P('section', None, None, 'head')
- grad_project_out: float32 [2, 768, 768], P('section', 'head')
- grad_branch_bias: float32 [2, 2, 768], P('section')
- grad_layer_scale: float32 [2, 2, 768], P('section')
- grad_expand_bias: float32 [2, 3072], P('section', 'head')
- grad_expand_weight: float32 [2, 768, 3072], P('section', None, 'head')
- grad_reduce_weight: float32 [2, 3072, 768], P('section', 'head')
Inputs may be any that keep to these rules, and one draw needn't show every extreme that they name: `images`: images are whole and contiguous within a slot: numbers never fall along a slot, and every slot holds one image of exactly 1024 tokens beside smaller ones.
All inputs are finite; a program needn't handle non-finite values.
Results may differ from a plain program's by a relative error of at most 0.018.
Values may be sent and summed in bfloat16 or wider, within the bound.
No kernel may reach another device: no remote copies, remote signals or barrier semaphores. Data moves between devices by JAX's collectives and lax.ppermute only.
A program may use at most 192 MiB of HBM per device.

v0:
```python
import jax
import jax.numpy as jnp
from jax import lax
from jax.sharding import PartitionSpec as P

HEAD_DIM = 64


norm_eps = 1e-06
masked_score = -1e30
root_half = 0.7071067811865476
inv_root_tau = 0.3989422804014327


def from_behind(shard, axis, by):
    devices = lax.axis_size(axis)
    pairs = [(i, i + by) for i in range(devices) if 0 <= i + by < devices]
    return lax.ppermute(shard, axis, pairs)


def for_sending(shard):

    def short(part):
        return part.astype(jnp.bfloat16) if part.dtype == jnp.float32 else part

    return jax.tree.map(short, shard)


def swapped(block, axis, distance):
    count = lax.axis_size(axis)
    route = []
    for low in range(count):
        high = low | 1 << distance
        if high != low and high < count:
            route += [(low, high), (high, low)]
    return lax.ppermute(block, axis, route)


def normalize(stream, gain_row, shift_row):
    center = stream - jnp.mean(stream, axis=-1, keepdims=True)
    inv_dev = lax.rsqrt(jnp.mean(center * center, axis=-1, keepdims=True) + norm_eps)
    unit_rows = center * inv_dev
    return (unit_rows * gain_row + shift_row, unit_rows, inv_dev)


def normalize_back(grad_rows, unit_rows, inv_dev, gain_row):
    scaled = grad_rows * gain_row
    inner = scaled - jnp.mean(scaled, axis=-1, keepdims=True)
    inner = inner - unit_rows * jnp.mean(scaled * unit_rows, axis=-1, keepdims=True)
    return (inv_dev * inner, jnp.sum(grad_rows * unit_rows, axis=0), jnp.sum(grad_rows, axis=0))


def gather_rows(rows):
    return lax.all_gather(rows, "head", axis=0, tiled=True)


def gather_grads(rows):
    return lax.all_gather(rows, "head", axis=0, tiled=True)


def branch_sum(values, weight):
    return lax.psum_scatter(
        jnp.dot(values, weight, preferred_element_type=jnp.float32).astype(jnp.bfloat16),
        "head",
        scatter_dimension=0,
        tiled=True,
    ).astype(jnp.float32)


def norm_grad_sum(grad_list, weight_list):
    share_rows = grad_list[0].shape[0] // lax.axis_size("head")
    running = jnp.zeros((share_rows * lax.axis_size("head"), weight_list[0].shape[0]), jnp.float32)
    for grad_rows, weight in zip(grad_list, weight_list):
        running = running + lax.dot_general(
            grad_rows, weight, (((1,), (1,)), ((), ())), preferred_element_type=jnp.float32
        )
    return lax.psum_scatter(
        running.astype(jnp.bfloat16), "head", scatter_dimension=0, tiled=True
    ).astype(jnp.float32)


def split_heads(values, head_count):
    return values.reshape(values.shape[0], head_count, values.shape[1] // head_count)


def masked_scores(query_block, key_heads, seg_block, segment_ids):
    scores = jnp.einsum("qhc,khc->hqk", query_block, key_heads, preferred_element_type=jnp.float32)
    scores = scores * query_block.shape[2] ** (-0.5)
    same_image = (seg_block[:, None] == segment_ids[None, :])[None]
    return jnp.where(same_image, scores, masked_score)


def attend(query_rows, key_rows, value_rows, segment_ids, head_count):
    total_rows = query_rows.shape[0]
    block_rows = min(512, total_rows)
    block_count = total_rows // block_rows
    key_heads = split_heads(key_rows, head_count)
    value_heads = split_heads(value_rows, head_count)
    queries = split_heads(query_rows, head_count).reshape(block_count, block_rows, head_count, -1)
    seg_blocks = segment_ids.reshape(block_count, block_rows)

    def block_step(item_pair):
        query_block, seg_block = item_pair
        scores = masked_scores(query_block, key_heads, seg_block, segment_ids)
        row_top = jnp.max(scores, axis=-1, keepdims=True)
        logsum = row_top + jnp.log(jnp.sum(jnp.exp(scores - row_top), axis=-1, keepdims=True))
        attn_probs = jnp.exp(scores - logsum).astype(jnp.bfloat16)
        mixed = jnp.einsum(
            "hqk,khc->qhc", attn_probs, value_heads, preferred_element_type=jnp.float32
        )
        return (mixed.astype(jnp.bfloat16).reshape(block_rows, -1), logsum)

    mixed, logsum = lax.map(block_step, (queries, seg_blocks))
    return (mixed.reshape(total_rows, -1), logsum)


def attend_back(query_rows, key_rows, value_rows, segment_ids, logsum, grad_mixed, head_count):
    total_rows = query_rows.shape[0]
    block_rows = min(512, total_rows)
    block_count = total_rows // block_rows
    head_size = query_rows.shape[1] // head_count
    score_scale = head_size ** (-0.5)
    key_heads = split_heads(key_rows, head_count)
    value_heads = split_heads(value_rows, head_count)
    queries = split_heads(query_rows, head_count).reshape(
        block_count, block_rows, head_count, head_size
    )
    grad_blocks = split_heads(grad_mixed, head_count).reshape(
        block_count, block_rows, head_count, head_size
    )
    seg_blocks = segment_ids.reshape(block_count, block_rows)

    def block_step(carried, item_quad):
        key_sum, value_sum = carried
        query_block, seg_block, lse_block, grad_block = item_quad
        scores = masked_scores(query_block, key_heads, seg_block, segment_ids)
        soft_probs = jnp.exp(scores - lse_block)
        attn_probs = soft_probs.astype(jnp.bfloat16)
        grad_probs = jnp.einsum(
            "qhc,khc->hqk", grad_block, value_heads, preferred_element_type=jnp.float32
        )
        row_delta = jnp.sum(grad_probs * soft_probs, axis=-1, keepdims=True)
        grad_scores = (soft_probs * (grad_probs - row_delta)).astype(jnp.bfloat16)
        grad_query = jnp.einsum(
            "hqk,khc->qhc", grad_scores, key_heads, preferred_element_type=jnp.float32
        )
        grad_query = (grad_query * score_scale).astype(jnp.bfloat16)
        key_sum = (
            key_sum
            + jnp.einsum(
                "hqk,qhc->khc", grad_scores, query_block, preferred_element_type=jnp.float32
            )
            * score_scale
        )
        value_sum = value_sum + jnp.einsum(
            "hqk,qhc->khc", attn_probs, grad_block, preferred_element_type=jnp.float32
        )
        return ((key_sum, value_sum), grad_query.reshape(block_rows, -1))

    zero_heads = jnp.zeros((total_rows, head_count, head_size), jnp.float32)
    sums, grad_query = lax.scan(
        block_step, (zero_heads, zero_heads), (queries, seg_blocks, logsum, grad_blocks)
    )
    grad_key = sums[0].astype(jnp.bfloat16).reshape(total_rows, -1)
    grad_value = sums[1].astype(jnp.bfloat16).reshape(total_rows, -1)
    return (grad_query.reshape(total_rows, -1), grad_key, grad_value)


def layer_forward(stream, segment_ids, weights):
    (
        gain_rows,
        shift_rows,
        input_bias,
        project_in,
        project_out,
        branch_bias,
        layer_scale,
        expand_bias,
        expand_weight,
        reduce_weight,
    ) = weights
    head_count = project_in.shape[2] // HEAD_DIM
    normed_one, unit_one, inv_one = normalize(stream, gain_rows[0], shift_rows[0])
    rows_one = gather_rows(normed_one.astype(jnp.bfloat16))
    projected = jnp.einsum("sd,jdc->jsc", rows_one, project_in, preferred_element_type=jnp.float32)
    query_rows = (projected[0] + input_bias[0]).astype(jnp.bfloat16)
    key_rows = projected[1].astype(jnp.bfloat16)
    value_rows = (projected[2] + input_bias[1]).astype(jnp.bfloat16)
    mixed, logsum = attend(query_rows, key_rows, value_rows, segment_ids, head_count)
    branch_one = branch_sum(mixed, project_out)
    middle = stream + layer_scale[0] * (branch_one + branch_bias[0])
    normed_two, unit_two, inv_two = normalize(middle, gain_rows[1], shift_rows[1])
    rows_two = gather_rows(normed_two.astype(jnp.bfloat16))
    hidden = jnp.dot(rows_two, expand_weight, preferred_element_type=jnp.float32) + expand_bias
    active = jax.nn.gelu(hidden, approximate=False).astype(jnp.bfloat16)
    branch_two = branch_sum(active, reduce_weight)
    result = middle + layer_scale[1] * (branch_two + branch_bias[1])
    kept_state = (
        unit_one,
        inv_one,
        rows_one,
        query_rows,
        key_rows,
        value_rows,
        mixed,
        logsum,
        branch_one,
        unit_two,
        inv_two,
        rows_two,
        hidden,
        active,
        branch_two,
    )
    return (result, kept_state)


def layer_backward(grad_out, segment_ids, weights, kept_state):
    (
        gain_rows,
        shift_rows,
        input_bias,
        project_in,
        project_out,
        branch_bias,
        layer_scale,
        expand_bias,
        expand_weight,
        reduce_weight,
    ) = weights
    (
        unit_one,
        inv_one,
        rows_one,
        query_rows,
        key_rows,
        value_rows,
        mixed,
        logsum,
        branch_one,
        unit_two,
        inv_two,
        rows_two,
        hidden,
        active,
        branch_two,
    ) = kept_state
    head_count = project_in.shape[2] // HEAD_DIM
    contract_rows = (((0,), (0,)), ((), ()))
    contract_cols = (((1,), (1,)), ((), ()))
    grad_scale_two = jnp.sum(grad_out * (branch_two + branch_bias[1]), axis=0)
    grad_bias_two = jnp.sum(grad_out, axis=0) * layer_scale[1]
    grad_branch_two = gather_grads((grad_out * layer_scale[1]).astype(jnp.bfloat16))
    grad_reduce = lax.dot_general(
        active, grad_branch_two, contract_rows, preferred_element_type=jnp.float32
    )
    grad_active = lax.dot_general(
        grad_branch_two, reduce_weight, contract_cols, preferred_element_type=jnp.float32
    )
    gelu_slope = 0.5 * (1.0 + lax.erf(hidden * root_half)) + hidden * inv_root_tau * jnp.exp(
        -0.5 * hidden * hidden
    )
    grad_hidden = (grad_active * gelu_slope).astype(jnp.bfloat16)
    grad_expand_bias = jnp.sum(grad_hidden.astype(jnp.float32), axis=0)
    grad_expand = lax.dot_general(
        rows_two, grad_hidden, contract_rows, preferred_element_type=jnp.float32
    )
    grad_normed_two = norm_grad_sum((grad_hidden,), (expand_weight,))
    back_two, grad_gain_two, grad_shift_two = normalize_back(
        grad_normed_two, unit_two, inv_two, gain_rows[1]
    )
    grad_middle = grad_out + back_two
    grad_scale_one = jnp.sum(grad_middle * (branch_one + branch_bias[0]), axis=0)
    grad_bias_one = jnp.sum(grad_middle, axis=0) * layer_scale[0]
    grad_branch_one = gather_grads((grad_middle * layer_scale[0]).astype(jnp.bfloat16))
    grad_project_out = lax.dot_general(
        mixed, grad_branch_one, contract_rows, preferred_element_type=jnp.float32
    )
    grad_mixed = lax.dot_general(
        grad_branch_one, project_out, contract_cols, preferred_element_type=jnp.float32
    ).astype(jnp.bfloat16)
    grad_query, grad_key, grad_value = attend_back(
        query_rows, key_rows, value_rows, segment_ids, logsum, grad_mixed, head_count
    )
    grad_stacked = jnp.stack((grad_query, grad_key, grad_value))
    grad_project_in = jnp.einsum(
        "sd,jsc->jdc", rows_one, grad_stacked, preferred_element_type=jnp.float32
    )
    grad_input_bias = jnp.stack(
        (
            jnp.sum(grad_query.astype(jnp.float32), axis=0),
            jnp.sum(grad_value.astype(jnp.float32), axis=0),
        )
    )
    grad_normed_one = norm_grad_sum(
        (grad_query, grad_key, grad_value), (project_in[0], project_in[1], project_in[2])
    )
    back_one, grad_gain_one, grad_shift_one = normalize_back(
        grad_normed_one, unit_one, inv_one, gain_rows[0]
    )
    grad_input = grad_middle + back_one
    grad_large = (
        grad_input_bias,
        grad_project_in,
        grad_project_out,
        grad_expand_bias,
        grad_expand,
        grad_reduce,
    )
    grad_small = (
        jnp.stack((grad_gain_one, grad_gain_two)),
        jnp.stack((grad_shift_one, grad_shift_two)),
        jnp.stack((grad_bias_one, grad_bias_two)),
        jnp.stack((grad_scale_one, grad_scale_two)),
    )
    return (grad_input, grad_large, grad_small)


def body(
    tokens,
    images,
    norm_gain,
    norm_shift,
    input_bias,
    project_in,
    project_out,
    branch_bias,
    layer_scale,
    expand_bias,
    expand_weight,
    reduce_weight,
    cotangent,
):
    weights = (
        norm_gain[0],
        norm_shift[0],
        input_bias[0],
        project_in[0],
        project_out[0],
        branch_bias[0],
        layer_scale[0],
        expand_bias[0],
        expand_weight[0],
        reduce_weight[0],
    )
    micro_count = tokens.shape[1]
    section_index = lax.axis_index("section")
    first_section = section_index == 0
    arriving = jnp.zeros(tokens.shape[2:], jnp.float32)
    kept_list = []
    finals = []
    for tick_index in range(micro_count + 1):
        own_rows = tokens[0, min(tick_index, micro_count - 1)].astype(jnp.float32)
        stream = jnp.where(first_section, own_rows, arriving)
        slot_index = jnp.clip(tick_index - section_index, 0, micro_count - 1)
        segment_ids = lax.dynamic_index_in_dim(images[0], slot_index, 0, keepdims=False)
        result, kept_state = layer_forward(stream, segment_ids, weights)
        kept_list.append((segment_ids, kept_state))
        low_result = result.astype(jnp.bfloat16)
        if tick_index >= 1:
            finals.append(low_result)
        if tick_index < micro_count:
            arriving = from_behind(low_result, "section", 1).astype(jnp.float32)
    backing = jnp.zeros(tokens.shape[2:], jnp.float32)
    large_total = None
    small_total = None
    grads_in = []
    for tick_index in range(micro_count + 1):
        usable = jnp.where(first_section, tick_index >= 1, tick_index <= micro_count - 1).astype(
            jnp.float32
        )
        given_rows = cotangent[0, max(micro_count - 1 - tick_index, 0)].astype(jnp.float32)
        grad_out = jnp.where(first_section, backing, given_rows)
        segment_ids, saved_state = kept_list[micro_count - tick_index]
        kept_state = saved_state
        grad_input, grad_large, grad_small = layer_backward(
            grad_out, segment_ids, weights, kept_state
        )
        grad_large = tuple((member * usable for member in grad_large))
        grad_small = tuple((member * usable for member in grad_small))
        if large_total is None:
            large_total = grad_large
            small_total = grad_small
        else:
            large_total = jax.tree.map(jnp.add, large_total, grad_large)
            small_total = jax.tree.map(jnp.add, small_total, grad_small)
        low_input = grad_input.astype(jnp.bfloat16)
        if tick_index >= 1:
            grads_in.append(low_input)
        if tick_index < micro_count:
            backing = from_behind(low_input, "section", -1).astype(jnp.float32)
    large_total = jax.tree.map(
        lambda part: part.astype(jnp.float32), lax.psum(for_sending(large_total), "dp")
    )
    small_total = lax.psum(small_total, ("head", "dp"))
    half_count = micro_count // 2
    final_stack = jnp.stack(finals)
    input_stack = jnp.stack(grads_in[::-1])
    outgoing = jnp.where(first_section, input_stack[half_count:], final_stack[:half_count])
    received = swapped(outgoing, "section", 0)
    final_tokens = jnp.where(first_section, received, final_stack[half_count:])[None]
    grad_tokens = jnp.where(first_section, input_stack[:half_count], received)[None]
    (
        grad_input_bias,
        grad_project_in,
        grad_project_out,
        grad_expand_bias,
        grad_expand,
        grad_reduce,
    ) = large_total
    grad_gain, grad_shift, grad_bias, grad_scale = small_total
    return (
        final_tokens,
        grad_tokens,
        grad_gain[None],
        grad_shift[None],
        grad_input_bias[None],
        grad_project_in[None],
        grad_project_out[None],
        grad_bias[None],
        grad_scale[None],
        grad_expand_bias[None],
        grad_expand[None],
        grad_reduce[None],
    )


def solution(mesh):
    return jax.shard_map(
        body,
        mesh=mesh,
        in_specs=(
            P("dp", None, "head", None),
            P("dp", None, None),
            P("section", None, None),
            P("section", None, None),
            P("section", None, "head"),
            P("section", None, None, "head"),
            P("section", "head", None),
            P("section", None, None),
            P("section", None, None),
            P("section", "head"),
            P("section", None, "head"),
            P("section", "head", None),
            P("dp", None, "head", None),
        ),
        out_specs=(
            P("dp", "section", "head", None),
            P("dp", "section", "head", None),
            P("section", None, None),
            P("section", None, None),
            P("section", None, "head"),
            P("section", None, None, "head"),
            P("section", "head", None),
            P("section", None, None),
            P("section", None, None),
            P("section", "head"),
            P("section", None, "head"),
            P("section", "head", None),
        ),
        check_vma=False,
    )
```

profile of v0, /device:TPU:0, one launch (start us, length us, event | category | flops | bytes accessed | tf_op | source)
XLA Modules:
  0.0 1592.0 jit_solution(11941518617735274597)
XLA Ops:
  14.0 26.0 %all-gather.13.cloned.1.call-done = bf16[1536,768]{1,0:T(8,128)(2,1)} async-done(((bf16[384,768]{1,0:T(8,128)(2,1)}), bf16[1536,768]{1,0:T(8,128)(2,1)}) %all-gather.13.cloned.1.call-update) | async-done | bytes 2359312 | tf_op jit(solution)/shard_map/all_gather | solution.py:54
  49.1 26.4 %while.81 = (s32[]{:T(128)}, bf16[3,512,192]{1,2,0:T(8,128)(2,1)}, f32[3,3,512,1]{2,1,3,0:T(4,128)S(1)}, s32[3,512]{1,0:T(4,128)S(1)}, s32[1536]{0:T(1024)S(1)},...) while((s32[]{:T(128)}, bf16[3,512,192]{1,2,0:T(8,128)(2,1)}, ...), condition=%wide.region_5.6_spmd, body=%wide.region_2.5_spmd.sunk | while | flops 630815232 | bytes 33493108 | solution.py:113
  80.4 33.0 %reduce-scatter.13.cloned.1.call-done = bf16[384,768]{1,0:T(8,128)(2,1)} async-done(((bf16[1536,768]{1,0:T(8,128)(2,1)}), bf16[384,768]{1,0:T(8,128)(2,1)}) %reduce-scatter.13.cloned.1.call-update) | async-done | bytes 589840 | tf_op jit(solution)/shard_map/reduce_scatter | solution.py:62
  161.0 33.2 %reduce-scatter.15.cloned.1.call-done = bf16[384,768]{1,0:T(8,128)(2,1)} async-done(((bf16[1536,768]{1,0:T(8,128)(2,1)}), bf16[384,768]{1,0:T(8,128)(2,1)}) %reduce-scatter.15.cloned.1.call-update) | async-done | bytes 589840 | tf_op jit(solution)/shard_map/reduce_scatter | solution.py:62
  214.6 24.4 %all-gather.17.cloned.1.call-done = bf16[1536,768]{1,0:T(8,128)(2,1)} async-done(((bf16[384,768]{1,0:T(8,128)(2,1)}), bf16[1536,768]{1,0:T(8,128)(2,1)}) %all-gather.17.cloned.1.call-update) | async-done | bytes 2359312 | tf_op jit(solution)/shard_map/all_gather | solution.py:54
  250.6 33.0 %while.82 = (s32[]{:T(128)}, bf16[3,512,192]{1,2,0:T(8,128)(2,1)}, f32[3,3,512,1]{2,1,3,0:T(4,128)}, s32[3,512]{1,0:T(4,128)}, s32[1536]{0:T(1024)S(1)}, /*index...) while((s32[]{:T(128)}, bf16[3,512,192]{1,2,0:T(8,128)(2,1)}, ...), condition=%wide.region_15.16_spmd, body=%wide.region_12.15_spmd.sunk | while | flops 630815232 | bytes 33486964 | solution.py:113
  289.2 33.2 %reduce-scatter.17.cloned.1.call-done = bf16[384,768]{1,0:T(8,128)(2,1)} async-done(((bf16[1536,768]{1,0:T(8,128)(2,1)}), bf16[384,768]{1,0:T(8,128)(2,1)}) %reduce-scatter.17.cloned.1.call-update) | async-done | bytes 589840 | tf_op jit(solution)/shard_map/reduce_scatter | solution.py:62
  369.5 33.2 %reduce-scatter.19.cloned.1.call-done = bf16[384,768]{1,0:T(8,128)(2,1)} async-done(((bf16[1536,768]{1,0:T(8,128)(2,1)}), bf16[384,768]{1,0:T(8,128)(2,1)}) %reduce-scatter.19.cloned.1.call-update) | async-done | bytes 589840 | tf_op jit(solution)/shard_map/reduce_scatter | solution.py:62
  423.7 24.4 %all-gather.21.cloned.1.call-done = bf16[1536,768]{1,0:T(8,128)(2,1)} async-done(((bf16[384,768]{1,0:T(8,128)(2,1)}), bf16[1536,768]{1,0:T(8,128)(2,1)}) %all-gather.21.cloned.1.call-update) | async-done | bytes 2359312 | tf_op jit(solution)/shard_map/all_gather | solution.py:54
  460.8 33.0 %while.83 = (s32[]{:T(128)}, bf16[3,512,192]{1,2,0:T(8,128)(2,1)}, f32[3,3,512,1]{2,1,3,0:T(4,128)}, s32[3,512]{1,0:T(4,128)}, s32[1536]{0:T(1024)S(1)}, /*index...) while((s32[]{:T(128)}, bf16[3,512,192]{1,2,0:T(8,128)(2,1)}, ...), condition=%wide.region_25.26_spmd, body=%wide.region_22.25_spmd.sunk | while | flops 630815232 | bytes 35846288 | solution.py:113
  499.0 33.1 %reduce-scatter.21.cloned.1.call-done = bf16[384,768]{1,0:T(8,128)(2,1)} async-done(((bf16[1536,768]{1,0:T(8,128)(2,1)}), bf16[384,768]{1,0:T(8,128)(2,1)}) %reduce-scatter.21.cloned.1.call-update) | async-done | bytes 589840 | tf_op jit(solution)/shard_map/reduce_scatter | solution.py:62
  597.7 33.2 %reduce-scatter.23.cloned.1.call-done = bf16[384,768]{1,0:T(8,128)(2,1)} async-done(((bf16[1536,768]{1,0:T(8,128)(2,1)}), bf16[384,768]{1,0:T(8,128)(2,1)}) %reduce-scatter.23.cloned.1.call-update) | async-done | bytes 589840 | tf_op jit(solution)/shard_map/reduce_scatter | solution.py:77
  668.9 95.0 %while.84 = (s32[]{:T(128)}, f32[1536,3,64]{0,2,1:T(8,128)}, f32[1536,3,64]{0,2,1:T(8,128)S(1)}, bf16[3,512,192]{1,2,0:T(8,128)(2,1)}, bf16[3,512,3,64]{1,3,2,0:...) while((s32[]{:T(128)}, f32[1536,3,64]{0,2,1:T(8,128)}, ...), condition=%wide.region_34.35_spmd.clone, body=%wide.region_32.34_spmd.clone.sunk | while | flops 1533639168 | bytes 139241744 | solution.py:161
  771.4 33.2 %reduce-scatter.25.cloned.1.call-done = bf16[384,768]{1,0:T(8,128)(2,1)} async-done(((bf16[1536,768]{1,0:T(8,128)(2,1)}), bf16[384,768]{1,0:T(8,128)(2,1)}) %reduce-scatter.25.cloned.1.call-update) | async-done | bytes 589840 | tf_op jit(solution)/shard_map/reduce_scatter | solution.py:77
  862.8 33.2 %reduce-scatter.27.cloned.1.call-done = bf16[384,768]{1,0:T(8,128)(2,1)} async-done(((bf16[1536,768]{1,0:T(8,128)(2,1)}), bf16[384,768]{1,0:T(8,128)(2,1)}) %reduce-scatter.27.cloned.1.call-update) | async-done | bytes 589840 | tf_op jit(solution)/shard_map/reduce_scatter | solution.py:77
  934.2 95.3 %while.85 = (s32[]{:T(128)}, f32[1536,3,64]{0,2,1:T(8,128)}, f32[1536,3,64]{0,2,1:T(8,128)S(1)}, bf16[3,512,192]{1,2,0:T(8,128)(2,1)}, bf16[3,512,3,64]{1,3,2,0:...) while((s32[]{:T(128)}, f32[1536,3,64]{0,2,1:T(8,128)}, ...), condition=%wide.region_43.44_spmd.clone, body=%wide.region_41.43_spmd.clone.sunk | while | flops 1533639168 | bytes 139241744 | solution.py:161
  1043.8 26.3 %reduce-scatter.29.cloned.1.call-done = bf16[384,768]{1,0:T(8,128)(2,1)} async-done(((bf16[1536,768]{1,0:T(8,128)(2,1)}), bf16[384,768]{1,0:T(8,128)(2,1)}) %reduce-scatter.29.cloned.1.call-update) | async-done | bytes 589840 | tf_op jit(solution)/shard_map/reduce_scatter | solution.py:77
  1076.9 28.9 %reduce-scatter.31.cloned.1.call-done = bf16[384,768]{1,0:T(8,128)(2,1)} async-done(((bf16[1536,768]{1,0:T(8,128)(2,1)}), bf16[384,768]{1,0:T(8,128)(2,1)}) %reduce-scatter.31.cloned.1.call-update) | async-done | bytes 589840 | tf_op jit(solution)/shard_map/reduce_scatter | solution.py:62
  1110.2 24.2 %all-gather.33.cloned.1.call-done = bf16[1536,768]{1,0:T(8,128)(2,1)} async-done(((bf16[384,768]{1,0:T(8,128)(2,1)}), bf16[1536,768]{1,0:T(8,128)(2,1)}) %all-gather.33.cloned.1.call-update) | async-done | bytes 2359312 | tf_op jit(solution)/shard_map/all_gather | solution.py:58
  1151.8 27.2 %reduce-scatter.33.cloned.1.call-done = bf16[384,768]{1,0:T(8,128)(2,1)} async-done(((bf16[1536,768]{1,0:T(8,128)(2,1)}), bf16[384,768]{1,0:T(8,128)(2,1)}) %reduce-scatter.33.cloned.1.call-update) | async-done | bytes 589840 | tf_op jit(solution)/shard_map/reduce_scatter | solution.py:77
  1233.8 95.5 %while.86 = (s32[]{:T(128)}, f32[1536,3,64]{0,2,1:T(8,128)}, f32[1536,3,64]{0,2,1:T(8,128)S(1)}, bf16[3,512,192]{1,2,0:T(8,128)(2,1)}, bf16[3,512,3,64]{1,3,2,0:...) while((s32[]{:T(128)}, f32[1536,3,64]{0,2,1:T(8,128)}, ...), condition=%wide.region_53.54_spmd.clone, body=%wide.region_51.53_spmd.clone.sunk | while | flops 1533639168 | bytes 139241744 | solution.py:161
  1390.6 89.2 %all-reduce.5.cloned.1.call-done = (bf16[1,3,768,192]{2,3,1,0:T(8,128)(2,1)}, bf16[1,192,768]{2,1,0:T(8,128)(2,1)}, bf16[1,768,768]{2,1,0:T(8,128)(2,1)}, bf16[1,768,768]{2,1,0:T(8,128)(2,1)}) async-done(((bf16[1,3,768,192]{2,3,1,0:T(8,128)(2,1)}, bf16[1,192,768]{2,1,0:T(8,128)(2,1)}, bf16[1,768,768]{2,1,0:T(8,128)(2,1)}, bf16[1,768,768]{2,1,0:T(8,128)(2,1)}), (bf16[1,3,768,192]{2,3,1,0:T(8,128)(2,1)}, ...) | async-done | bytes 3538960 | tf_op jit(solution)/shard_map/psum | solution.py:393
  1487.4 27.0 %reduce-scatter.35.cloned.1.call-done = bf16[384,768]{1,0:T(8,128)(2,1)} async-done(((bf16[1536,768]{1,0:T(8,128)(2,1)}), bf16[384,768]{1,0:T(8,128)(2,1)}) %reduce-scatter.35.cloned.1.call-update) | async-done | bytes 589840 | tf_op jit(solution)/shard_map/reduce_scatter | solution.py:77
  1519.4 60.6 %all-reduce = (f32[1,2,768]{2,1,0:T(2,128)}, f32[1,2,768]{2,1,0:T(2,128)}, f32[1,2,768]{2,1,0:T(2,128)}, f32[1,2,768]{2,1,0:T(2,128)}) all-reduce(f32[1,2,768]{2,1,0:T(2,128)} %fusion.293, f32[1,2,768]{2,1,0:T(2,128)} %fusion.296, f32[1,2,768]{2,1,0:T(2,128)} %fusion.299, ...), channel_id=1, replica_groups=mesh['section'=2,'head'=4,'dp'=4] {'head','dp'}, use_global_device_ids=true, to_apply=%region_63.64 | all-reduce | flops 6144 | bytes 49152 | tf_op jit(solution)/shard_map/psum | solution.py:395
  (827 shorter events, 951.7 us)
Async XLA Ops:
  13.1 100.4 %reduce-scatter.13.cloned.1.call-start = ((), (), s32[]{:S(2)}) async-start(), calls=%async_computation.13 | async-start | bytes 2949120 | tf_op jit(solution)/shard_map/reduce_scatter | solution.py:62
  80.3 61.7 %all-gather.15.cloned.1.call-start = ((), (), s32[]{:S(2)}) async-start(), calls=%async_computation.14 | async-start | bytes 2949120 | tf_op jit(solution)/shard_map/all_gather | solution.py:54
  117.8 76.4 %reduce-scatter.15.cloned.1.call-start = ((), (), s32[]{:S(2)}) async-start(), calls=%async_computation.15 | async-start | bytes 2949120 | tf_op jit(solution)/shard_map/reduce_scatter | solution.py:62
  160.9 78.0 %all-gather.17.cloned.1.call-start = ((), (), s32[]{:S(2)}) async-start(), calls=%async_computation.16 | async-start | bytes 2949120 | tf_op jit(solution)/shard_map/all_gather | solution.py:54
  213.7 108.7 %reduce-scatter.17.cloned.1.call-start = ((), (), s32[]{:S(2)}) async-start(), calls=%async_computation.17 | async-start | bytes 2949120 | tf_op jit(solution)/shard_map/reduce_scatter | solution.py:62
  289.1 61.5 %all-gather.19.cloned.1.call-start = ((), (), s32[]{:S(2)}) async-start(), calls=%async_computation.18 | async-start | bytes 2949120 | tf_op jit(solution)/shard_map/all_gather | solution.py:54
  326.4 76.3 %reduce-scatter.19.cloned.1.call-start = ((), (), s32[]{:S(2)}) async-start(), calls=%async_computation.19 | async-start | bytes 2949120 | tf_op jit(solution)/shard_map/reduce_scatter | solution.py:62
  369.5 78.7 %all-gather.21.cloned.1.call-start = ((), (), s32[]{:S(2)}) async-start(), calls=%async_computation.20 | async-start | bytes 2949120 | tf_op jit(solution)/shard_map/all_gather | solution.py:54
  422.9 109.3 %reduce-scatter.21.cloned.1.call-start = ((), (), s32[]{:S(2)}) async-start(), calls=%async_computation.21 | async-start | bytes 2949120 | tf_op jit(solution)/shard_map/reduce_scatter | solution.py:62
  499.0 61.0 %all-gather.25.cloned.1.call-start = ((), (), s32[]{:S(2)}) async-start(), calls=%async_computation.23 | async-start | bytes 2949120 | tf_op jit(solution)/shard_map/all_gather | solution.py:54
  536.4 94.5 %reduce-scatter.23.cloned.1.call-start = ((), (), s32[]{:S(2)}) async-start(), calls=%async_computation.24 | async-start | bytes 2949120 | tf_op jit(solution)/shard_map/reduce_scatter | solution.py:77
  597.6 62.8 %all-gather.27.cloned.1.call-start = ((), (), s32[]{:S(2)}) async-start(), calls=%async_computation.25 | async-start | bytes 2949120 | tf_op jit(solution)/shard_map/all_gather | solution.py:58
  636.2 168.4 %reduce-scatter.25.cloned.1.call-start = ((), (), s32[]{:S(2)}) async-start(), calls=%async_computation.26 | async-start | bytes 2949120 | tf_op jit(solution)/shard_map/reduce_scatter | solution.py:77
  771.4 79.9 %all-gather.29.cloned.1.call-start = ((), (), s32[]{:S(2)}) async-start(), calls=%async_computation.27 | async-start | bytes 2949120 | tf_op jit(solution)/shard_map/all_gather | solution.py:58
  828.0 68.0 %reduce-scatter.27.cloned.1.call-start = ((), (), s32[]{:S(2)}) async-start(), calls=%async_computation.28 | async-start | bytes 2949120 | tf_op jit(solution)/shard_map/reduce_scatter | solution.py:77
  862.7 62.8 %all-gather.31.cloned.1.call-start = ((), (), s32[]{:S(2)}) async-start(), calls=%async_computation.29 | async-start | bytes 2949120 | tf_op jit(solution)/shard_map/all_gather | solution.py:58
  901.3 168.8 %reduce-scatter.29.cloned.1.call-start = ((), (), s32[]{:S(2)}) async-start(), calls=%async_computation.30 | async-start | bytes 2949120 | tf_op jit(solution)/shard_map/reduce_scatter | solution.py:77
  1036.9 68.9 %reduce-scatter.31.cloned.1.call-start = ((), (), s32[]{:S(2)}) async-start(), calls=%async_computation.31 | async-start | bytes 2949120 | tf_op jit(solution)/shard_map/reduce_scatter | solution.py:62
  1043.4 91.0 %all-gather.33.cloned.1.call-start = ((), (), s32[]{:S(2)}) async-start(), calls=%async_computation.32 | async-start | bytes 2949120 | tf_op jit(solution)/shard_map/all_gather | solution.py:58
  1110.1 68.9 %reduce-scatter.33.cloned.1.call-start = ((), (), s32[]{:S(2)}) async-start(), calls=%async_computation.33 | async-start | bytes 2949120 | tf_op jit(solution)/shard_map/reduce_scatter | solution.py:77
  1145.8 79.3 %all-gather.35.cloned.1.call-start = ((), (), s32[]{:S(2)}) async-start(), calls=%async_computation.34 | async-start | bytes 2949120 | tf_op jit(solution)/shard_map/all_gather | solution.py:58
  1186.7 293.0 %all-reduce.5.cloned.1.call-start = ((), (), s32[]{:S(2)}) async-start(), calls=%async_computation.36 | async-start | bytes 7077888 | tf_op jit(solution)/shard_map/psum | solution.py:393
  1344.6 169.9 %reduce-scatter.35.cloned.1.call-start = ((), (), s32[]{:S(2)}) async-start(), calls=%async_computation.35 | async-start | bytes 2949120 | tf_op jit(solution)/shard_map/reduce_scatter | solution.py:77
  1365.2 216.2 %collective-permute-start.3 = (bf16[1,384,768]{2,1,0:T(8,128)(2,1)}, bf16[1,384,768]{2,1,0:T(8,128)(2,1)}, u32[]{:S(2)}, u32[]{:S(2)}) collective-permute-start(bf16[1,384,768]{2,1,0:T(8,128)(2,1)} %get-tuple-element.722), channel_id=1, source_target_pairs={{0,16},{16,0},{1,17},{17,1},{2,18},{18,2},{3,19},{19,3},{4,20},{20... | collective-permute-start | bytes 1769480 | tf_op jit(solution)/shard_map/ppermute | solution.py:36
  (205 other events, 5061.9 us)
Sparse Core Ops, SparseCore 0:
  13.2 26.7 all-gather.12
  80.4 33.0 reduce-scatter.12
  117.9 24.0 all-gather.14
  161.0 33.0 reduce-scatter.14
  213.8 25.1 all-gather.16
  289.2 33.0 reduce-scatter.16
  326.6 24.0 all-gather.18
  369.6 33.0 reduce-scatter.18
  423.0 25.0 all-gather.20
  499.1 33.0 reduce-scatter.20
  535.9 24.0 all-gather.24
  562.1 24.0 all-gather.22
  597.7 33.0 reduce-scatter.22
  636.3 24.0 all-gather.26
  771.5 33.0 reduce-scatter.24
  862.8 33.0 reduce-scatter.26
  901.4 24.0 all-gather.30
  1037.0 33.0 reduce-scatter.28
  1072.7 33.0 reduce-scatter.30
  1110.2 24.0 all-gather.32
  1145.9 33.0 reduce-scatter.32
  1186.8 24.0 all-gather.34
  1344.7 135.0 all-reduce.4
  1482.4 31.9 reduce-scatter.34
  (1 shorter events, 23.1 us)
where the time goes:
time: 1600 us; the launch traced here: 1590 us
  waiting for transfers between devices  759 us (47%)
  matrix products  369 us (23%)
  other arithmetic  214 us (13%)
  local copies, waits for them, and re-layouts  146 us (9%)
  blocking collectives  73.1 us (5%)
    reduce_scatter x6, waiting for transfers between devices, branch_sum(): lax.psum_scatter(jnp.dot(values, weight, preferred_element_type=jnp.float...  195 us
    reduce_scatter x6, waiting for transfers between devices, norm_grad_sum(): lax.psum_scatter(running.astype(jnp.bfloat16), 'head', scatter_dimension=...  180 us
    all_gather x6, waiting for transfers between devices, gather_rows(): return lax.all_gather(rows, 'head', axis=0, tiled=True)  146 us
    all_gather x6, waiting for transfers between devices, gather_grads(): return lax.all_gather(rows, 'head', axis=0, tiled=True)  107 us
    psum x1, waiting for transfers between devices, body(): lax.psum(for_sending(large_total), 'dp')  89.2 us
    convert_element_type x9, other arithmetic, block_step(): grad_scores = (soft_probs * (grad_probs - row_delta)).astype(jnp.bfloat16)  84.9 us
    psum x1, blocking collectives, body(): small_total = lax.psum(small_total, ('head', 'dp'))  60.6 us
    dot_general x18, matrix products, masked_scores(): jnp.einsum('qhc,khc->hqk', query_block, key_heads, preferred_element_type...  56.3 us
  transfers between devices with their start and end apart: 30, of which 27 were waited for; matrix products, arithmetic and copies ran while one was open for 7% of the time, Pallas kernels for 0%

commit v1 on v0

v1 whole, which is shorter than its diff:
```python
import functools
import jax
import jax.numpy as jnp
from jax import lax
from jax.experimental import pallas as pl
from jax.experimental.pallas import tpu as pltpu
from jax.sharding import PartitionSpec as P

HEAD_DIM = 64
LANES = 128
norm_eps = 1e-06
masked_score = -1e30
root_half = 0.7071067811865476
inv_root_tau = 0.3989422804014327
f32 = jnp.float32
bf16 = jnp.bfloat16


def swap(x, axis, mask):
    n = lax.axis_size(axis)
    return lax.ppermute(x, axis, [(i, i ^ mask) for i in range(n)])


def swap_chip(x):
    return swap(x, "head", 2)


def swap_core(x):
    return swap(x, "head", 1)


def swap_section(x):
    return swap(x, "section", 1)


def dot(a, b):
    return jnp.dot(a, b, preferred_element_type=f32)


def dot_t(a, b):
    return lax.dot_general(a, b, (((1,), (1,)), ((), ())), preferred_element_type=f32)


def dot_rows(a, b):
    return lax.dot_general(a, b, (((0,), (0,)), ((), ())), preferred_element_type=f32)


def normalize(stream, gain, shift):
    center = stream - jnp.mean(stream, axis=-1, keepdims=True)
    inv_dev = lax.rsqrt(jnp.mean(center * center, axis=-1, keepdims=True) + norm_eps)
    unit = center * inv_dev
    return (unit * gain + shift).astype(bf16), unit, inv_dev


def normalize_back(grad, unit, inv_dev, gain):
    scaled = grad * gain
    inner = scaled - jnp.mean(scaled, axis=-1, keepdims=True)
    inner = inner - unit * jnp.mean(scaled * unit, axis=-1, keepdims=True)
    return inv_dev * inner, jnp.sum(grad * unit, axis=0), jnp.sum(grad, axis=0)


def attn_fwd_kernel(qr, kr, q_ref, k_ref, v_ref, sq_ref, sk_ref, o_ref, lse_ref, m_ref, l_ref, acc_ref, *, qb, kb):
    pairs = q_ref.shape[1] // LANES
    nk = k_ref.shape[0] // kb
    i = pl.program_id(0)
    m_ref[...] = jnp.full_like(m_ref, -3e38)
    l_ref[...] = jnp.zeros_like(l_ref)
    acc_ref[...] = jnp.zeros_like(acc_ref)
    lane = lax.broadcasted_iota(jnp.int32, (qb, LANES), 1)
    lo, hi = qr[0, i], qr[1, i]
    for j in range(nk):
        @pl.when(jnp.logical_and(kr[0, j] <= hi, kr[1, j] >= lo))
        def _():
            bias = jnp.where(sk_ref[pl.ds(j * kb, kb), :] == sq_ref[...], 0.0, masked_score)
            for p in range(pairs):
                cols = pl.ds(p * LANES, LANES)
                kblk = k_ref[pl.ds(j * kb, kb), cols]
                vblk = v_ref[pl.ds(j * kb, kb), cols]
                qblk = q_ref[:, cols]
                for e in range(2):
                    h = 2 * p + e
                    qm = jnp.where((lane < HEAD_DIM) == (e == 0), qblk, jnp.zeros_like(qblk))
                    s = dot_t(kblk, qm) + bias
                    top = m_ref[h:h + 1, :]
                    new = jnp.maximum(top, jnp.max(s, axis=0, keepdims=True))
                    alpha = jnp.exp(top - new)
                    pr = jnp.exp(s - new)
                    l_ref[h:h + 1, :] = l_ref[h:h + 1, :] * alpha + jnp.sum(pr, axis=0, keepdims=True)
                    m_ref[h:h + 1, :] = new
                    ov = dot_rows(vblk, pr.astype(bf16))
                    rows = pl.ds(h * HEAD_DIM, HEAD_DIM)
                    acc_ref[rows, :] = acc_ref[rows, :] * alpha + ov[e * HEAD_DIM:(e + 1) * HEAD_DIM, :]
    for h in range(2 * pairs):
        rows = pl.ds(h * HEAD_DIM, HEAD_DIM)
        acc_ref[rows, :] = acc_ref[rows, :] / l_ref[h:h + 1, :]
    o_ref[...] = acc_ref[...].T.astype(bf16)
    lse_ref[...] = m_ref[...] + jnp.log(jnp.maximum(l_ref[...], 1e-37))


def attend(q, k, v, seg_q, seg_k, qb=128, kb=384):
    rows, width = q.shape
    keys = k.shape[0]
    heads = width // HEAD_DIM
    qs = seg_q.reshape(rows // qb, qb)
    ks = seg_k.reshape(keys // kb, kb)
    qr = jnp.stack([qs[:, 0], qs[:, -1]])
    kr = jnp.stack([ks[:, 0], ks[:, -1]])
    return pl.pallas_call(
        functools.partial(attn_fwd_kernel, qb=qb, kb=kb),
        grid_spec=pltpu.PrefetchScalarGridSpec(
            num_scalar_prefetch=2,
            grid=(rows // qb,),
            in_specs=[
                pl.BlockSpec((qb, width), lambda i, *_: (i, 0)),
                pl.BlockSpec((keys, width), lambda i, *_: (0, 0)),
                pl.BlockSpec((keys, width), lambda i, *_: (0, 0)),
                pl.BlockSpec((1, qb), lambda i, *_: (0, i)),
                pl.BlockSpec((keys, 1), lambda i, *_: (0, 0)),
            ],
            out_specs=[
                pl.BlockSpec((qb, width), lambda i, *_: (i, 0)),
                pl.BlockSpec((8, qb), lambda i, *_: (0, i)),
            ],
            scratch_shapes=[
                pltpu.VMEM((8, qb), f32),
                pltpu.VMEM((8, qb), f32),
                pltpu.VMEM((width, qb), f32),
            ],
        ),
        out_shape=[
            jax.ShapeDtypeStruct((rows, width), bf16),
            jax.ShapeDtypeStruct((8, rows), f32),
        ],
        name="attn_fwd",
    )(qr, kr, q, k, v, seg_q.reshape(1, rows), seg_k.reshape(keys, 1))


def attn_bwd_kernel(qr, kr, q_ref, k_ref, v_ref, g_ref, o_ref, lse_ref, sq_ref, sk_ref, gq_ref, gk_ref, gv_ref, gqa_ref, *, qb, kb):
    pairs = q_ref.shape[1] // LANES
    nk = k_ref.shape[0] // kb
    i = pl.program_id(0)

    @pl.when(i == 0)
    def _():
        gk_ref[...] = jnp.zeros_like(gk_ref)
        gv_ref[...] = jnp.zeros_like(gv_ref)

    gqa_ref[...] = jnp.zeros_like(gqa_ref)
    lane = lax.broadcasted_iota(jnp.int32, (qb, LANES), 1)
    picks = lax.broadcasted_iota(jnp.int32, (8, LANES), 1)
    lo, hi = qr[0, i], qr[1, i]
    deltas = []
    for p in range(pairs):
        cols = pl.ds(p * LANES, LANES)
        prod = g_ref[:, cols].astype(f32) * o_ref[:, cols].astype(f32)
        for e in range(2):
            pick = jnp.where((picks < HEAD_DIM) == (e == 0), 1.0, 0.0)
            both = lax.dot_general(pick, prod, (((1,), (1,)), ((), ())), precision=lax.Precision.HIGHEST, preferred_element_type=f32)
            deltas.append(both[0:1, :])
    for j in range(nk):
        @pl.when(jnp.logical_and(kr[0, j] <= hi, kr[1, j] >= lo))
        def _():
            krows = pl.ds(j * kb, kb)
            same = sk_ref[krows, :] == sq_ref[...]
            bias = jnp.where(same, 0.0, masked_score)
            for p in range(pairs):
                cols = pl.ds(p * LANES, LANES)
                kblk = k_ref[krows, cols]
                vblk = v_ref[krows, cols]
                qblk = q_ref[:, cols]
                gblk = g_ref[:, cols]
                gk_new, gv_new, gq_new = 0.0, 0.0, 0.0
                for e in range(2):
                    h = 2 * p + e
                    mine = (lane < HEAD_DIM) == (e == 0)
                    qm = jnp.where(mine, qblk, jnp.zeros_like(qblk))
                    gm = jnp.where(mine, gblk, jnp.zeros_like(gblk))
                    s = dot_t(kblk, qm) + bias
                    pr = jnp.exp(s - lse_ref[h:h + 1, :])
                    gp = dot_t(vblk, gm)
                    gs = (pr * (gp - deltas[h])).astype(bf16)
                    gv_new = gv_new + dot(pr.astype(bf16), gm)
                    gk_new = gk_new + dot(gs, qm)
                    gq_new = gq_new + jnp.where(mine, dot_rows(gs, kblk), 0.0)
                gv_ref[krows, cols] += gv_new
                gk_ref[krows, cols] += gk_new
                gqa_ref[:, cols] += gq_new
    gq_ref[...] = (gqa_ref[...] * HEAD_DIM ** -0.5).astype(bf16)


def attend_back(q, k, v, seg_q, seg_k, g, o, lse, qb=128, kb=384):
    rows, width = q.shape
    keys = k.shape[0]
    qs = seg_q.reshape(rows // qb, qb)
    ks = seg_k.reshape(keys // kb, kb)
    qr = jnp.stack([qs[:, 0], qs[:, -1]])
    kr = jnp.stack([ks[:, 0], ks[:, -1]])
    qspec = pl.BlockSpec((qb, width), lambda i, *_: (i, 0))
    kspec = pl.BlockSpec((keys, width), lambda i, *_: (0, 0))
    return pl.pallas_call(
        functools.partial(attn_bwd_kernel, qb=qb, kb=kb),
        grid_spec=pltpu.PrefetchScalarGridSpec(
            num_scalar_prefetch=2,
            grid=(rows // qb,),
            in_specs=[
                qspec, kspec, kspec, qspec, qspec,
                pl.BlockSpec((8, qb), lambda i, *_: (0, i)),
                pl.BlockSpec((1, qb), lambda i, *_: (0, i)),
                pl.BlockSpec((keys, 1), lambda i, *_: (0, 0)),
            ],
            out_specs=[qspec, kspec, kspec],
            scratch_shapes=[pltpu.VMEM((qb, width), f32)],
        ),
        out_shape=[
            jax.ShapeDtypeStruct((rows, width), bf16),
            jax.ShapeDtypeStruct((keys, width), f32),
            jax.ShapeDtypeStruct((keys, width), f32),
        ],
        name="attn_bwd",
    )(qr, kr, q, k, v, g, o, lse, seg_q.reshape(1, rows), seg_k.reshape(keys, 1))


def gelu_parts(u):
    cdf = 0.5 * (1.0 + lax.erf(u * root_half))
    slope = cdf + u * inv_root_tau * jnp.exp(-0.5 * u * u)
    return (u * cdf).astype(bf16), slope.astype(bf16)


def layer_forward(stream, segs, w):
    seg_q, seg_k = segs
    width = w["out"].shape[0]
    n1, unit1, inv1 = normalize(stream, w["gain"][0], w["shift"][0])
    n1 = jnp.concatenate([n1, swap_chip(n1)])
    qkv = (dot(n1, w["in"]) + w["in_bias"]).astype(bf16)
    own = n1.shape[0] // 2
    q = qkv[:, :width] * jnp.bfloat16(HEAD_DIM ** -0.5)
    kv = qkv[:, width:]
    kv = jnp.concatenate([kv, swap_core(kv)])
    k, v = kv[:, :width], kv[:, width:]
    mixed, lse = attend(q, k, v, seg_q, seg_k)
    branch1 = dot(mixed[:own], w["out"]) + swap_chip(dot(mixed[own:], w["out"]).astype(bf16)).astype(f32)
    branch1 = branch1 + w["bias"][0]
    middle = stream + w["scale"][0] * branch1
    n2, unit2, inv2 = normalize(middle, w["gain"][1], w["shift"][1])
    n2r = swap_chip(n2)
    act_o, slope_o = gelu_parts(dot(n2, w["expand"]) + w["expand_bias"])
    act_r, slope_r = gelu_parts(dot(n2r, w["expand"]) + w["expand_bias"])
    back = swap_chip(dot(act_r, w["reduce"]).astype(bf16))
    branch2 = dot(act_o, w["reduce"]) + back.astype(f32) + w["bias"][1]
    result = middle + w["scale"][1] * branch2
    kept = (n1, unit1, inv1, q, k, v, mixed, lse, branch1, n2, n2r, unit2, inv2, act_o, slope_o, act_r, slope_r, branch2)
    return result, kept


def layer_backward(g_out, segs, w, kept):
    n1, unit1, inv1, q, k, v, mixed, lse, branch1, n2, n2r, unit2, inv2, act_o, slope_o, act_r, slope_r, branch2 = kept
    seg_q, seg_k = segs
    own = n2.shape[0]
    g_scale2 = jnp.sum(g_out * branch2, axis=0)
    g_bias2 = jnp.sum(g_out, axis=0) * w["scale"][1]
    gb2 = (g_out * w["scale"][1]).astype(bf16)
    gb2r = swap_chip(gb2)
    gh_o = (dot_t(gb2, w["reduce"]) * slope_o.astype(f32)).astype(bf16)
    gh_r = (dot_t(gb2r, w["reduce"]) * slope_r.astype(f32)).astype(bf16)
    back = swap_chip(dot_t(gh_r, w["expand"]).astype(bf16))
    g_n2 = dot_t(gh_o, w["expand"]) + back.astype(f32)
    g_reduce = dot_rows(act_o, gb2) + dot_rows(act_r, gb2r)
    g_expand = dot_rows(n2, gh_o) + dot_rows(n2r, gh_r)
    g_expand_bias = jnp.sum(gh_o.astype(f32), axis=0) + jnp.sum(gh_r.astype(f32), axis=0)
    back2, g_gain2, g_shift2 = normalize_back(g_n2, unit2, inv2, w["gain"][1])
    g_mid = g_out + back2
    g_scale1 = jnp.sum(g_mid * branch1, axis=0)
    g_bias1 = jnp.sum(g_mid, axis=0) * w["scale"][0]
    gb1 = (g_mid * w["scale"][0]).astype(bf16)
    gb1 = jnp.concatenate([gb1, swap_chip(gb1)])
    g_out_w = dot_rows(mixed, gb1)
    g_mixed = dot_t(gb1, w["out"]).astype(bf16)
    gq, gk, gv = attend_back(q, k, v, seg_q, seg_k, g_mixed, mixed, lse)
    half = 2 * own
    other = swap_core(jnp.concatenate([gk[half:], gv[half:]], axis=1).astype(bf16))
    gkv = (jnp.concatenate([gk[:half], gv[:half]], axis=1) + other.astype(f32)).astype(bf16)
    g_qkv = jnp.concatenate([gq, gkv], axis=1)
    g_in_w = dot_rows(n1, g_qkv)
    g_in_bias = jnp.sum(g_qkv.astype(f32), axis=0)
    back = swap_chip(dot_t(g_qkv[own:], w["in"]).astype(bf16))
    g_n1 = dot_t(g_qkv[:own], w["in"]) + back.astype(f32)
    back1, g_gain1, g_shift1 = normalize_back(g_n1, unit1, inv1, w["gain"][0])
    g_in = g_mid + back1
    small = jnp.stack([g_gain1, g_gain2, g_shift1, g_shift2, g_bias1, g_bias2, g_scale1, g_scale2])
    large = {"in": g_in_w, "in_bias": g_in_bias, "out": g_out_w, "expand": g_expand, "expand_bias": g_expand_bias, "reduce": g_reduce}
    return g_in, large, small


def body(tokens, images, norm_gain, norm_shift, input_bias, project_in, project_out, branch_bias, layer_scale, expand_bias, expand_weight, reduce_weight, cotangent):
    section = lax.axis_index("section")
    head = lax.axis_index("head")
    core = head % 2
    first = section == 0
    quarter = project_in.shape[3]
    own = {
        "in": project_in[0].transpose(1, 0, 2).reshape(project_in.shape[2], -1),
        "out": project_out[0],
        "expand": expand_weight[0],
        "reduce": reduce_weight[0],
        "small": jnp.concatenate([norm_gain[0], norm_shift[0], branch_bias[0], layer_scale[0]]),
        "vec": jnp.concatenate([input_bias[0].reshape(-1), expand_bias[0]]),
    }
    other = jax.tree.map(swap_section, own)
    layers = []
    for layer in range(2):
        mine = first if layer == 0 else jnp.logical_not(first)
        a = jax.tree.map(lambda x, y: jnp.where(mine, x, y), own, other)
        b = {name: swap_core(a[name]) for name in ("in", "out", "expand", "reduce", "vec")}
        parts = []
        even = {name: jnp.where(core == 0, a[name], b[name]) for name in ("in", "out", "vec")}
        odd = {name: jnp.where(core == 0, b[name], a[name]) for name in ("in", "out", "vec")}
        for j in range(3):
            cols = slice(j * quarter, (j + 1) * quarter)
            parts += [even["in"][:, cols], odd["in"][:, cols]]
        zero = jnp.zeros((2 * quarter,), f32)
        w = {
            "in": jnp.concatenate(parts, axis=1),
            "out": jnp.concatenate([even["out"], odd["out"]]),
            "expand": jnp.concatenate([a["expand"], b["expand"]], axis=1),
            "reduce": jnp.concatenate([a["reduce"], b["reduce"]]),
            "gain": a["small"][0:2], "shift": a["small"][2:4], "bias": a["small"][4:6], "scale": a["small"][6:8],
            "in_bias": jnp.concatenate([even["vec"][:quarter], odd["vec"][:quarter], zero, even["vec"][quarter:2 * quarter], odd["vec"][quarter:2 * quarter]]),
            "expand_bias": jnp.concatenate([a["vec"][2 * quarter:], b["vec"][2 * quarter:]]),
        }
        layers.append(w)
    pieces = lax.dynamic_index_in_dim(images[0], section, 0, keepdims=False).reshape(lax.axis_size("head"), -1)
    order = [lax.dynamic_index_in_dim(pieces, head ^ mask, 0, keepdims=False) for mask in (0, 2, 1, 3)]
    segs = (jnp.concatenate(order[:2]), jnp.concatenate(order))
    stream = lax.dynamic_index_in_dim(tokens[0], section, 0, keepdims=False).astype(f32)
    result, kept0 = layer_forward(stream, segs, layers[0])
    result, kept1 = layer_forward(result.astype(bf16).astype(f32), segs, layers[1])
    final_tokens = result.astype(bf16)
    g_out = lax.dynamic_index_in_dim(cotangent[0], section, 0, keepdims=False).astype(f32)
    g_in, large1, small1 = layer_backward(g_out, segs, layers[1], kept1)
    g_in, large0, small0 = layer_backward(g_in.astype(bf16).astype(f32), segs, layers[0], kept0)
    grad_tokens = g_in.astype(bf16)

    def by_core(large):
        mine, theirs = {}, {}
        w = 2 * quarter
        mine["in"] = jnp.stack([large["in"][:, j * w:j * w + quarter] for j in range(3)])
        theirs["in"] = jnp.stack([large["in"][:, j * w + quarter:(j + 1) * w] for j in range(3)])
        mine["in_bias"] = jnp.stack([large["in_bias"][j * w:j * w + quarter] for j in (0, 2)])
        theirs["in_bias"] = jnp.stack([large["in_bias"][j * w + quarter:(j + 1) * w] for j in (0, 2)])
        mine["out"], theirs["out"] = jnp.split(large["out"], 2)
        for name in ("in", "in_bias", "out"):
            even, odd = mine[name], theirs[name]
            mine[name], theirs[name] = jnp.where(core == 0, even, odd), jnp.where(core == 0, odd, even)
        for name, axis in (("expand", 1), ("expand_bias", 0), ("reduce", 0)):
            mine[name], theirs[name] = jnp.split(large[name], 2, axis=axis)
        return {name: mine[name] + swap_core(theirs[name].astype(bf16)).astype(f32) for name in mine}

    large0, large1 = by_core(large0), by_core(large1)
    total = {}
    for name in large0:
        send = jnp.where(first, large1[name], large0[name]).astype(bf16)
        keep = jnp.where(first, large0[name], large1[name])
        total[name] = (keep + swap_section(send).astype(f32)).astype(bf16)
    total = {name: part.astype(f32) for name, part in lax.psum(total, "dp").items()}
    small = lax.psum(jnp.stack([small0, small1]), ("section", "head", "dp"))
    small = lax.dynamic_index_in_dim(small, section, 0, keepdims=False)
    return (
        final_tokens[None, None],
        grad_tokens[None, None],
        small[None, 0:2],
        small[None, 2:4],
        total["in_bias"][None],
        total["in"][None],
        total["out"][None],
        small[None, 4:6],
        small[None, 6:8],
        total["expand_bias"][None],
        total["expand"][None],
        total["reduce"][None],
    )


def solution(mesh):
    return jax.shard_map(
        body,
        mesh=mesh,
        in_specs=(
            P("dp", None, "head", None),
            P("dp", None, None),
            P("section", None, None),
            P("section", None, None),
            P("section", None, "head"),
            P("section", None, None, "head"),
            P("section", "head", None),
            P("section", None, None),
            P("section", None, None),
            P("section", "head"),
            P("section", None, "head"),
            P("section", "head", None),
            P("dp", None, "head", None),
        ),
        out_specs=(
            P("dp", "section", "head", None),
            P("dp", "section", "head", None),
            P("section", None, None),
            P("section", None, None),
            P("section", None, "head"),
            P("section", None, None, "head"),
            P("section", "head", None),
            P("section", None, None),
            P("section", None, None),
            P("section", "head"),
            P("section", None, "head"),
            P("section", "head", None),
        ),
        check_vma=False,
    )
```

time: 1600 us -> 730 us (0.46)
  waiting for transfers between devices: 759 us -> 265 us
  matrix products: 369 us -> 82.7 us
  other arithmetic: 214 us -> 80.6 us
  local copies, waits for them, and re-layouts: 146 us -> 40 us
  Pallas kernels: 0 us -> 93.8 us
  starting transfers between devices: 15 us -> 91.4 us
  blocking collectives: 73.1 us -> 53.9 us
    reduce_scatter x12 -> x0, waiting for transfers between devices: 375 us -> none  [the longest x6 195 us: branch_sum(): lax.psum_scatter(jnp.dot(values, weight, preferred_element_type=jnp.float...]
    dot_general x102 -> x40, matrix products: 359 us -> 82.7 us  [the longest x14 37.3 us: dot_t(): lax.dot_general(a, b, (((1,), (1,)), ((), ())), preferred_element_type=f32)]
    all_gather x12 -> x0, waiting for transfers between devices: 253 us -> none  [the longest x6 146 us: gather_rows(): return lax.all_gather(rows, 'head', axis=0, tiled=True)]
    ppermute x5 -> x54, waiting for transfers between devices: 40.7 us -> 211 us  [swap(): return lax.ppermute(x, axis, [(i, i ^ mask) for i in range(n)])]
    convert_element_type x32 -> x23, other arithmetic: 116 us -> 16.9 us  [the longest x6 9.18 us: body(): send = jnp.where(first, large1[name], large0[name]).astype(bf16)]
    pallas_call x0 -> x4, Pallas kernels: none -> 93.8 us  [the longest x2 65.8 us: attend_back(): pl.pallas_call(functools.partial(attn_bwd_kernel, qb=qb, kb=kb), grid_spe...]
    ppermute x5 -> x54, starting transfers between devices: 11.4 us -> 91.4 us  [swap(): return lax.ppermute(x, axis, [(i, i ^ mask) for i in range(n)])]
    reduce_sum x24 -> x6, other arithmetic: 52.7 us -> 7.28 us  [the longest x2 3.28 us: layer_backward(): g_scale1 = jnp.sum(g_mid * branch1, axis=0)]
  transfers between devices with their start and end apart: 30 -> 55, of which waited for: 27 -> 22; matrix products, arithmetic and copies ran while one was open for 7% -> 22% of each run, Pallas kernels for 0% -> 6%
where the time goes in v1:
time: 730 us; the launch traced here: 724 us
  waiting for transfers between devices  265 us (36%)
  Pallas kernels  93.8 us (13%)
  starting transfers between devices  91.4 us (13%)
  matrix products  82.7 us (11%)
  other arithmetic  80.6 us (11%)
  blocking collectives  53.9 us (7%)
  local copies, waits for them, and re-layouts  40 us (5%)
  between operations  16.8 us (2%)
    ppermute x54, waiting for transfers between devices, swap(): return lax.ppermute(x, axis, [(i, i ^ mask) for i in range(n)])  211 us
    ppermute x54, starting transfers between devices, swap(): return lax.ppermute(x, axis, [(i, i ^ mask) for i in range(n)])  91.4 us
    pallas_call x2, Pallas kernels, attend_back(): pl.pallas_call(functools.partial(attn_bwd_kernel, qb=qb, kb=kb), grid_spe...  65.8 us
    psum x1, waiting for transfers between devices, body(): lax.psum(total, 'dp').items()  53.7 us
    psum x1, blocking collectives, body(): small = lax.psum(jnp.stack([small0, small1]), ('section', 'head', 'dp'))  40.8 us
    dot_general x14, matrix products, dot_t(): lax.dot_general(a, b, (((1,), (1,)), ((), ())), preferred_element_type=f32)  37.3 us
    pallas_call x2, Pallas kernels, attend(): pl.pallas_call(functools.partial(attn_fwd_kernel, qb=qb, kb=kb), grid_spe...  28.1 us
    dot_general x12, matrix products, dot_rows(): lax.dot_general(a, b, (((0,), (0,)), ((), ())), preferred_element_type=f32)  24.6 us
  transfers between devices with their start and end apart: 55, of which 22 were waited for; matrix products, arithmetic and copies ran while one was open for 22% of the time, Pallas kernels for 6%

profile of v1, /device:TPU:0, one launch (start us, length us, event | category | flops | bytes accessed | tf_op | source)
XLA Modules:
  0.0 724.4 jit_solution(642382869483034998)
XLA Ops:
  20.4 10.7 %collective-permute-done.4 = f32[1152]{0:T(1024)S(1)} collective-permute-done((f32[1152]{0:T(1024)S(1)}, f32[1152]{0:T(1024)S(1)}, u32[]{:S(2)}, u32[]{:S(2)}) %collective-permute-start.4) | collective-permute-done | bytes 4640 | tf_op jit(solution)/shard_map/ppermute | solution.py:21
  44.9 12.5 %collective-permute-done.1 = bf16[384,768]{1,0:T(8,128)(2,1)S(1)} collective-permute-done((bf16[384,768]{1,0:T(8,128)(2,1)S(1)}, bf16[384,768]{1,0:T(8,128)(2,1)S(1)}, u32[]{:S(2)}, u32[]{:S(2)}) %collective-permute-start.1) | collective-permute-done | bytes 589856 | tf_op jit(solution)/shard_map/ppermute | solution.py:21
  74.4 14.0 %attn_fwd.2 = (bf16[768,384]{1,0:T(8,128)(2,1)}, f32[8,768]{1,0:T(8,128)}) custom-call(s32[2,6]{1,0:T(2,128)} %pad_add_fusion.3.qr, s32[2,4]{1,0:T(2,128)} %pad_add_fusion.4.kr, bf16[768,384]{1,0:T(8,128)(2,1)} %slice_multiply_fusion.1.q_ref, bf16[1536,384]{1,0:T(8,128)(2,1)} %get-tuple-element.163.k_ref, bf16[1536,384]{1,0:T(8,128)(2,1)} %get-tuple-element.162.v_ref, ...), custom_call_target="tpu_custom_call" | custom-call | tf_op jit(solution)/shard_map/attn_fwd/pallas_call | solution.py:108
  108.0 10.9 %collective-permute-done.14 = bf16[384,768]{1,0:T(8,128)(2,1)S(1)} collective-permute-done((bf16[384,768]{1,0:T(8,128)(2,1)S(1)}, bf16[384,768]{1,0:T(8,128)(2,1)S(1)}, u32[]{:S(2)}, u32[]{:S(2)}) %collective-permute-start.14) | collective-permute-done | bytes 589856 | tf_op jit(solution)/shard_map/ppermute | solution.py:21
  125.8 10.5 %collective-permute-done.15 = bf16[384,768]{1,0:T(8,128)(2,1)S(1)} collective-permute-done((bf16[384,768]{1,0:T(8,128)(2,1)S(1)}, bf16[384,768]{1,0:T(8,128)(2,1)S(1)}, u32[]{:S(2)}, u32[]{:S(2)}) %collective-permute-start.15) | collective-permute-done | bytes 589856 | tf_op jit(solution)/shard_map/ppermute | solution.py:21
  141.1 14.3 %collective-permute-done.16 = bf16[384,768]{1,0:T(8,128)(2,1)S(1)} collective-permute-done((bf16[384,768]{1,0:T(8,128)(2,1)S(1)}, bf16[384,768]{1,0:T(8,128)(2,1)S(1)}, u32[]{:S(2)}, u32[]{:S(2)}) %collective-permute-start.16) | collective-permute-done | bytes 589856 | tf_op jit(solution)/shard_map/ppermute | solution.py:21
  163.4 14.1 %attn_fwd.3 = (bf16[768,384]{1,0:T(8,128)(2,1)}, f32[8,768]{1,0:T(8,128)}) custom-call(s32[2,6]{1,0:T(2,128)} %pad_add_fusion.3.qr, s32[2,4]{1,0:T(2,128)} %pad_add_fusion.4.kr, bf16[768,384]{1,0:T(8,128)(2,1)} %slice_multiply_fusion.q_ref, bf16[1536,384]{1,0:T(8,128)(2,1)} %get-tuple-element.161.k_ref, bf16[1536,384]{1,0:T(8,128)(2,1)} %get-tuple-element.160.v_ref, ...), custom_call_target="tpu_custom_call" | custom-call | tf_op jit(solution)/shard_map/attn_fwd/pallas_call | solution.py:108
  197.1 10.1 %collective-permute-done.24 = bf16[384,768]{1,0:T(8,128)(2,1)S(1)} collective-permute-done((bf16[384,768]{1,0:T(8,128)(2,1)S(1)}, bf16[384,768]{1,0:T(8,128)(2,1)S(1)}, u32[]{:S(2)}, u32[]{:S(2)}) %collective-permute-start.24) | collective-permute-done | bytes 589856 | tf_op jit(solution)/shard_map/ppermute | solution.py:21
  208.3 11.5 %collective-permute-done.26 = bf16[384,768]{1,0:T(8,128)(2,1)S(1)} collective-permute-done((bf16[384,768]{1,0:T(8,128)(2,1)S(1)}, bf16[384,768]{1,0:T(8,128)(2,1)S(1)}, u32[]{:S(2)}, u32[]{:S(2)}) %collective-permute-start.26) | collective-permute-done | bytes 589856 | tf_op jit(solution)/shard_map/ppermute | solution.py:21
  232.5 7.5 %collective-permute-done.27 = bf16[384,768]{1,0:T(8,128)(2,1)S(1)} collective-permute-done((bf16[384,768]{1,0:T(8,128)(2,1)S(1)}, bf16[384,768]{1,0:T(8,128)(2,1)S(1)}, u32[]{:S(2)}, u32[]{:S(2)}) %collective-permute-start.27) | collective-permute-done | bytes 589856 | tf_op jit(solution)/shard_map/ppermute | solution.py:21
  242.0 10.7 %collective-permute-done.25 = bf16[384,768]{1,0:T(8,128)(2,1)S(1)} collective-permute-done((bf16[384,768]{1,0:T(8,128)(2,1)S(1)}, bf16[384,768]{1,0:T(8,128)(2,1)S(1)}, u32[]{:S(2)}, u32[]{:S(2)}) %collective-permute-start.25) | collective-permute-done | bytes 589856 | tf_op jit(solution)/shard_map/ppermute | solution.py:21
  264.8 8.3 %collective-permute-done.28 = bf16[384,768]{1,0:T(8,128)(2,1)} collective-permute-done((bf16[384,768]{1,0:T(8,128)(2,1)}, bf16[384,768]{1,0:T(8,128)(2,1)}, u32[]{:S(2)}, u32[]{:S(2)}) %collective-permute-start.28) | collective-permute-done | bytes 589856 | tf_op jit(solution)/shard_map/ppermute | solution.py:21
  276.1 33.0 %attn_bwd.2 = (bf16[768,384]{1,0:T(8,128)(2,1)}, f32[1536,384]{1,0:T(8,128)}, f32[1536,384]{1,0:T(8,128)}) custom-call(s32[2,6]{1,0:T(2,128)} %pad_add_fusion.3.qr, s32[2,4]{1,0:T(2,128)} %pad_add_fusion.4.kr, bf16[768,384]{1,0:T(8,128)(2,1)} %slice_multiply_fusion.q_ref, bf16[1536,384]{1,0:T(8,128)(2,1)} %get-tuple-element.161.k_ref, ...), custom_call_target="tpu_custom_call" | custom-call | tf_op jit(solution)/shard_map/attn_bwd/pallas_call | solution.py:200
  312.0 10.6 %collective-permute-start.29 = (bf16[768,768]{1,0:T(8,128)(2,1)S(1)}, bf16[768,768]{1,0:T(8,128)(2,1)S(1)}, u32[]{:S(2)}, u32[]{:S(2)}) collective-permute-start(bf16[768,768]{1,0:T(8,128)(2,1)S(1)} %pad_maximum_fusion.15), channel_id=1, source_target_pairs={{0,4},{4,0},{8,12},{12,8},{1,5},{5,1},{9,13},{13,9},{2,6},{6,2},{1... | collective-permute-start | bytes 3538952 | tf_op jit(solution)/shard_map/ppermute | solution.py:21
  361.2 10.2 %collective-permute-done.31 = bf16[384,768]{1,0:T(8,128)(2,1)S(1)} collective-permute-done((bf16[384,768]{1,0:T(8,128)(2,1)S(1)}, bf16[384,768]{1,0:T(8,128)(2,1)S(1)}, u32[]{:S(2)}, u32[]{:S(2)}) %collective-permute-start.31) | collective-permute-done | bytes 589856 | tf_op jit(solution)/shard_map/ppermute | solution.py:21
  410.5 32.8 %attn_bwd.3 = (bf16[768,384]{1,0:T(8,128)(2,1)}, f32[1536,384]{1,0:T(8,128)}, f32[1536,384]{1,0:T(8,128)}) custom-call(s32[2,6]{1,0:T(2,128)} %pad_add_fusion.3.qr, s32[2,4]{1,0:T(2,128)} %pad_add_fusion.4.kr, bf16[768,384]{1,0:T(8,128)(2,1)} %slice_multiply_fusion.1.q_ref, bf16[1536,384]{1,0:T(8,128)(2,1)} %get-tuple-element.163.k_ref, ...), custom_call_target="tpu_custom_call" | custom-call | tf_op jit(solution)/shard_map/attn_bwd/pallas_call | solution.py:200
  446.5 8.1 %collective-permute-start.34 = (bf16[768,768]{1,0:T(8,128)(2,1)S(1)}, bf16[768,768]{1,0:T(8,128)(2,1)S(1)}, u32[]{:S(2)}, u32[]{:S(2)}) collective-permute-start(bf16[768,768]{1,0:T(8,128)(2,1)S(1)} %pad_maximum_fusion.17), channel_id=1, source_target_pairs={{0,4},{4,0},{8,12},{12,8},{1,5},{5,1},{9,13},{13,9},{2,6},{6,2},{1... | collective-permute-start | bytes 3538952 | tf_op jit(solution)/shard_map/ppermute | solution.py:21
  471.6 18.7 %collective-permute-start.53 = (bf16[768,768]{1,0:T(8,128)(2,1)S(1)}, bf16[768,768]{1,0:T(8,128)(2,1)S(1)}, u32[]{:S(2)}, u32[]{:S(2)}) collective-permute-start(bf16[768,768]{1,0:T(8,128)(2,1)S(1)} %copy-done.59), channel_id=1, source_target_pairs={{0,16},{16,0},{1,17},{17,1},{2,18},{18,2},{3,19},{19,3},{4,20},{20... | collective-permute-start | bytes 3538952 | tf_op jit(solution)/shard_map/ppermute | solution.py:21
  493.4 29.7 %collective-permute-done.44 = bf16[192,768]{1,0:T(8,128)(2,1)} collective-permute-done((bf16[192,768]{1,0:T(8,128)(2,1)S(1)}, bf16[192,768]{1,0:T(8,128)(2,1)}, u32[]{:S(2)}, u32[]{:S(2)}) %collective-permute-start.44) | collective-permute-done | bytes 294944 | tf_op jit(solution)/shard_map/ppermute | solution.py:21
  531.6 20.6 %collective-permute-done.50 = bf16[768,768]{1,0:T(8,128)(2,1)S(1)} collective-permute-done((bf16[768,768]{1,0:T(8,128)(2,1)}, bf16[768,768]{1,0:T(8,128)(2,1)S(1)}, u32[]{:S(2)}, u32[]{:S(2)}) %collective-permute-start.50) | collective-permute-done | bytes 1179680 | tf_op jit(solution)/shard_map/ppermute | solution.py:21
  555.4 14.7 %collective-permute-done.41 = bf16[3,768,192]{1,2,0:T(8,128)(2,1)} collective-permute-done((bf16[3,768,192]{1,2,0:T(8,128)(2,1)}, bf16[3,768,192]{1,2,0:T(8,128)(2,1)}, u32[]{:S(2)}, u32[]{:S(2)}) %collective-permute-start.41) | collective-permute-done | bytes 884768 | tf_op jit(solution)/shard_map/ppermute | solution.py:21
  589.8 13.2 %all-reduce = (bf16[1,2,192]{2,1,0:T(2,128)(2,1)}, bf16[1,768]{1,0:T(2,128)(2,1)}) all-reduce(bf16[1,2,192]{2,1,0:T(2,128)(2,1)S(1)} %fusion.95, bf16[1,768]{1,0:T(2,128)(2,1)} %broadcast_in_dim.76), channel_id=1, replica_groups=mesh['section'=2,'head'=4,'dp'=4] {'dp'}, use_global_device_ids=true, to_apply=%region_35.36 | all-reduce | flops 1152 | bytes 4608 | tf_op jit(solution)/shard_map/psum | solution.py:364
  611.4 40.8 %psum.49 = f32[2,8,768]{2,1,0:T(8,128)S(1)} all-reduce(f32[2,8,768]{2,1,0:T(8,128)S(1)} %pad_maximum_fusion.36), channel_id=1, replica_groups=mesh['section'=2,'head'=4,'dp'=4] {'section','head','dp'}, use_global_device_ids=true, to_apply=%region_32.33 | all-reduce | flops 12288 | bytes 98304 | tf_op jit(solution)/shard_map/psum | solution.py:365
  656.7 53.7 %all-reduce.4.cloned.1.call-done = (bf16[1,3,768,192]{2,3,1,0:T(8,128)(2,1)}, bf16[1,192,768]{2,1,0:T(8,128)(2,1)}, bf16[1,768,768]{2,1,0:T(8,128)(2,1)}, bf16[1,768,768]{2,1,0:T(8,128)(2,1)}) async-done(((bf16[1,3,768,192]{2,3,1,0:T(8,128)(2,1)}, bf16[1,192,768]{2,1,0:T(8,128)(2,1)}, bf16[1,768,768]{2,1,0:T(8,128)(2,1)}, bf16[1,768,768]{2,1,0:T(8,128)(2,1)}), (bf16[1,3,768,192]{2,3,1,0:T(8,128)(2,1)}, ...) | async-done | bytes 3538960 | tf_op jit(solution)/shard_map/psum | solution.py:364
  (674 shorter events, 286.6 us)
Async XLA Ops:
  7.2 703.1 %all-reduce.4.cloned.1.call-start = ((), (), s32[]{:S(2)}) async-start(), calls=%async_computation | async-start | bytes 7077888 | tf_op jit(solution)/shard_map/psum | solution.py:364
  7.2 29.0 %collective-permute-start.2 = (bf16[768,576]{0,1:T(8,128)(2,1)}, bf16[768,576]{0,1:T(8,128)(2,1)S(1)}, u32[]{:S(2)}, u32[]{:S(2)}) collective-permute-start(bf16[768,576]{0,1:T(8,128)(2,1)} %bitcast.171), channel_id=1, source_target_pairs={{0,16},{16,0},{1,17},{17,1},{2,18},{18,2},{3,19},{19,3},{4,20},{20... | collective-permute-start | bytes 2654216 | tf_op jit(solution)/shard_map/ppermute | solution.py:21
  12.6 27.6 %collective-permute-start = (f32[8,768]{1,0:T(8,128)S(1)}, f32[8,768]{1,0:T(8,128)S(1)}, u32[]{:S(2)}, u32[]{:S(2)}) collective-permute-start(f32[8,768]{1,0:T(8,128)S(1)} %pad_maximum_fusion.37), channel_id=1, source_target_pairs={{0,16},{16,0},{1,17},{17,1},{2,18},{18,2},{3,19},{19,3},{4,20},{20... | collective-permute-start | bytes 73736 | tf_op jit(solution)/shard_map/ppermute | solution.py:21
  14.6 44.7 %collective-permute-start.7 = (bf16[192,768]{1,0:T(8,128)(2,1)}, bf16[192,768]{1,0:T(8,128)(2,1)}, u32[]{:S(2)}, u32[]{:S(2)}) collective-permute-start(bf16[192,768]{1,0:T(8,128)(2,1)} %bitcast.172), channel_id=1, source_target_pairs={{0,16},{16,0},{1,17},{17,1},{2,18},{18,2},{3,19},{19,3},{4,20},{20... | collective-permute-start | bytes 884744 | tf_op jit(solution)/shard_map/ppermute | solution.py:21
  14.7 76.8 %collective-permute-start.10 = (bf16[768,768]{1,0:T(8,128)(2,1)}, bf16[768,768]{1,0:T(8,128)(2,1)}, u32[]{:S(2)}, u32[]{:S(2)}) collective-permute-start(bf16[768,768]{1,0:T(8,128)(2,1)} %bitcast.170), channel_id=1, source_target_pairs={{0,16},{16,0},{1,17},{17,1},{2,18},{18,2},{3,19},{19,3},{4,20},{20... | collective-permute-start | bytes 3538952 | tf_op jit(solution)/shard_map/ppermute | solution.py:21
  34.1 64.0 %collective-permute-start.12 = (bf16[768,768]{1,0:T(8,128)(2,1)}, bf16[768,768]{1,0:T(8,128)(2,1)}, u32[]{:S(2)}, u32[]{:S(2)}) collective-permute-start(bf16[768,768]{1,0:T(8,128)(2,1)} %bitcast.12), channel_id=1, source_target_pairs={{0,16},{16,0},{1,17},{17,1},{2,18},{18,2},{3,19},{19,3},{4,20},{20... | collective-permute-start | bytes 3538952 | tf_op jit(solution)/shard_map/ppermute | solution.py:21
  69.1 37.4 %collective-permute-start.17 = (bf16[768,576]{0,1:T(8,128)(2,1)S(1)}, bf16[768,576]{0,1:T(8,128)(2,1)}, u32[]{:S(2)}, u32[]{:S(2)}) collective-permute-start(bf16[768,576]{0,1:T(8,128)(2,1)S(1)} %get-tuple-element.167), channel_id=1, source_target_pairs={{0,4},{4,0},{8,12},{12,8},{1,5},{5,1},{9,13},{13,9},{2,6},{6,2},{1... | collective-permute-start | bytes 2654216 | tf_op jit(solution)/shard_map/ppermute | solution.py:21
  185.1 34.7 %collective-permute-start.23 = (bf16[768,768]{1,0:T(8,128)(2,1)S(1)}, bf16[768,768]{1,0:T(8,128)(2,1)S(1)}, u32[]{:S(2)}, u32[]{:S(2)}) collective-permute-start(bf16[768,768]{1,0:T(8,128)(2,1)S(1)} %copy-done.46), channel_id=1, source_target_pairs={{0,4},{4,0},{8,12},{12,8},{1,5},{5,1},{9,13},{13,9},{2,6},{6,2},{1... | collective-permute-start | bytes 3538952 | tf_op jit(solution)/shard_map/ppermute | solution.py:21
  195.2 24.6 %collective-permute-start.26 = (bf16[384,768]{1,0:T(8,128)(2,1)S(1)}, bf16[384,768]{1,0:T(8,128)(2,1)S(1)}, u32[]{:S(2)}, u32[]{:S(2)}) collective-permute-start(bf16[384,768]{1,0:T(8,128)(2,1)S(1)} %fusion.63), channel_id=1, source_target_pairs={{0,8},{4,12},{8,0},{12,4},{1,9},{5,13},{9,1},{13,5},{2,10},{6,14},... | collective-permute-start | bytes 1769480 | tf_op jit(solution)/shard_map/ppermute | solution.py:21
  232.1 20.5 %collective-permute-start.25 = (bf16[384,768]{1,0:T(8,128)(2,1)S(1)}, bf16[384,768]{1,0:T(8,128)(2,1)S(1)}, u32[]{:S(2)}, u32[]{:S(2)}) collective-permute-start(bf16[384,768]{1,0:T(8,128)(2,1)S(1)} %convolution_convert_fusion.2), channel_id=1, source_target_pairs={{0,8},{4,12},{8,0},{12,4},{1,9},{5,13},{9,1},{13,5},{2,10},{6,14},... | collective-permute-start | bytes 1769480 | tf_op jit(solution)/shard_map/ppermute | solution.py:21
  312.0 22.2 %collective-permute-start.29 = (bf16[768,768]{1,0:T(8,128)(2,1)S(1)}, bf16[768,768]{1,0:T(8,128)(2,1)S(1)}, u32[]{:S(2)}, u32[]{:S(2)}) collective-permute-start(bf16[768,768]{1,0:T(8,128)(2,1)S(1)} %pad_maximum_fusion.15), channel_id=1, source_target_pairs={{0,4},{4,0},{8,12},{12,8},{1,5},{5,1},{9,13},{13,9},{2,6},{6,2},{1... | collective-permute-start | bytes 3538952 | tf_op jit(solution)/shard_map/ppermute | solution.py:21
  326.7 132.2 %collective-permute-start.52 = (bf16[768,768]{1,0:T(8,128)(2,1)}, bf16[768,768]{1,0:T(8,128)(2,1)}, u32[]{:S(2)}, u32[]{:S(2)}) collective-permute-start(bf16[768,768]{1,0:T(8,128)(2,1)} %split.154), channel_id=1, source_target_pairs={{0,4},{4,0},{8,12},{12,8},{1,5},{5,1},{9,13},{13,9},{2,6},{6,2},{1... | collective-permute-start | bytes 3538952 | tf_op jit(solution)/shard_map/ppermute | solution.py:21
  330.8 139.8 %collective-permute-start.49 = (bf16[768,768]{1,0:T(8,128)(2,1)}, bf16[768,768]{1,0:T(8,128)(2,1)}, u32[]{:S(2)}, u32[]{:S(2)}) collective-permute-start(bf16[768,768]{1,0:T(8,128)(2,1)} %split.156), channel_id=1, source_target_pairs={{0,4},{4,0},{8,12},{12,8},{1,5},{5,1},{9,13},{13,9},{2,6},{6,2},{1... | collective-permute-start | bytes 3538952 | tf_op jit(solution)/shard_map/ppermute | solution.py:21
  332.9 240.6 %collective-permute-start.46 = (bf16[768]{0:T(1024)(128)(2,1)}, bf16[768]{0:T(1024)(128)(2,1)}, u32[]{:S(2)}, u32[]{:S(2)}) collective-permute-start(bf16[768]{0:T(1024)(128)(2,1)} %split.158), channel_id=1, source_target_pairs={{0,4},{4,0},{8,12},{12,8},{1,5},{5,1},{9,13},{13,9},{2,6},{6,2},{1... | collective-permute-start | bytes 4616 | tf_op jit(solution)/shard_map/ppermute | solution.py:21
  399.2 59.9 %collective-permute-start.51 = (bf16[768,768]{1,0:T(8,128)(2,1)}, bf16[768,768]{1,0:T(8,128)(2,1)S(1)}, u32[]{:S(2)}, u32[]{:S(2)}) collective-permute-start(bf16[768,768]{1,0:T(8,128)(2,1)} %split.155), channel_id=1, source_target_pairs={{0,4},{4,0},{8,12},{12,8},{1,5},{5,1},{9,13},{13,9},{2,6},{6,2},{1... | collective-permute-start | bytes 3538952 | tf_op jit(solution)/shard_map/ppermute | solution.py:21
  459.2 31.1 %collective-permute-start.48 = (bf16[768,768]{1,0:T(8,128)(2,1)S(1)}, bf16[768,768]{1,0:T(8,128)(2,1)S(1)}, u32[]{:S(2)}, u32[]{:S(2)}) collective-permute-start(bf16[768,768]{1,0:T(8,128)(2,1)S(1)} %split.157), channel_id=1, source_target_pairs={{0,4},{4,0},{8,12},{12,8},{1,5},{5,1},{9,13},{13,9},{2,6},{6,2},{1... | collective-permute-start | bytes 3538952 | tf_op jit(solution)/shard_map/ppermute | solution.py:21
  469.9 56.9 %collective-permute-start.40 = (bf16[3,768,192]{1,2,0:T(8,128)(2,1)}, bf16[3,768,192]{1,2,0:T(8,128)(2,1)S(1)}, u32[]{:S(2)}, u32[]{:S(2)}) collective-permute-start(bf16[3,768,192]{1,2,0:T(8,128)(2,1)} %select_convert_fusion.3), channel_id=1, source_target_pairs={{0,4},{4,0},{8,12},{12,8},{1,5},{5,1},{9,13},{13,9},{2,6},{6,2},{1... | collective-permute-start | bytes 2654216 | tf_op jit(solution)/shard_map/ppermute | solution.py:21
  470.2 56.6 %collective-permute-start.39 = (bf16[3,768,192]{1,2,0:T(8,128)(2,1)}, bf16[3,768,192]{1,2,0:T(8,128)(2,1)S(1)}, u32[]{:S(2)}, u32[]{:S(2)}) collective-permute-start(bf16[3,768,192]{1,2,0:T(8,128)(2,1)} %select_convert_fusion.4), channel_id=1, source_target_pairs={{0,4},{4,0},{8,12},{12,8},{1,5},{5,1},{9,13},{13,9},{2,6},{6,2},{1... | collective-permute-start | bytes 2654216 | tf_op jit(solution)/shard_map/ppermute | solution.py:21
  471.6 57.0 %collective-permute-start.53 = (bf16[768,768]{1,0:T(8,128)(2,1)S(1)}, bf16[768,768]{1,0:T(8,128)(2,1)S(1)}, u32[]{:S(2)}, u32[]{:S(2)}) collective-permute-start(bf16[768,768]{1,0:T(8,128)(2,1)S(1)} %copy-done.59), channel_id=1, source_target_pairs={{0,16},{16,0},{1,17},{17,1},{2,18},{18,2},{3,19},{19,3},{4,20},{20... | collective-permute-start | bytes 3538952 | tf_op jit(solution)/shard_map/ppermute | solution.py:21
  490.3 32.9 %collective-permute-start.44 = (bf16[192,768]{1,0:T(8,128)(2,1)S(1)}, bf16[192,768]{1,0:T(8,128)(2,1)}, u32[]{:S(2)}, u32[]{:S(2)}) collective-permute-start(bf16[192,768]{1,0:T(8,128)(2,1)S(1)} %select_convert_fusion.5), channel_id=1, source_target_pairs={{0,16},{16,0},{1,17},{17,1},{2,18},{18,2},{3,19},{19,3},{4,20},{20... | collective-permute-start | bytes 884744 | tf_op jit(solution)/shard_map/ppermute | solution.py:21
  523.1 29.1 %collective-permute-start.50 = (bf16[768,768]{1,0:T(8,128)(2,1)}, bf16[768,768]{1,0:T(8,128)(2,1)S(1)}, u32[]{:S(2)}, u32[]{:S(2)}) collective-permute-start(bf16[768,768]{1,0:T(8,128)(2,1)} %select_convert_fusion.1), channel_id=1, source_target_pairs={{0,16},{16,0},{1,17},{17,1},{2,18},{18,2},{3,19},{19,3},{4,20},{20... | collective-permute-start | bytes 3538952 | tf_op jit(solution)/shard_map/ppermute | solution.py:21
  526.8 46.7 %collective-permute-start.45 = (bf16[768]{0:T(1024)(128)(2,1)}, bf16[768]{0:T(1024)(128)(2,1)}, u32[]{:S(2)}, u32[]{:S(2)}) collective-permute-start(bf16[768]{0:T(1024)(128)(2,1)} %split.159), channel_id=1, source_target_pairs={{0,4},{4,0},{8,12},{12,8},{1,5},{5,1},{9,13},{13,9},{2,6},{6,2},{1... | collective-permute-start | bytes 4616 | tf_op jit(solution)/shard_map/ppermute | solution.py:21
  528.2 41.9 %collective-permute-start.41 = (bf16[3,768,192]{1,2,0:T(8,128)(2,1)}, bf16[3,768,192]{1,2,0:T(8,128)(2,1)}, u32[]{:S(2)}, u32[]{:S(2)}) collective-permute-start(bf16[3,768,192]{1,2,0:T(8,128)(2,1)} %select_convert_fusion.2), channel_id=1, source_target_pairs={{0,16},{16,0},{1,17},{17,1},{2,18},{18,2},{3,19},{19,3},{4,20},{20... | collective-permute-start | bytes 2654216 | tf_op jit(solution)/shard_map/ppermute | solution.py:21
  583.0 22.4 %collective-permute-start.35 = (bf16[384,768]{1,0:T(8,128)(2,1)}, bf16[384,768]{1,0:T(8,128)(2,1)}, u32[]{:S(2)}, u32[]{:S(2)}) collective-permute-start(bf16[384,768]{1,0:T(8,128)(2,1)} %convolution_convert_fusion.4), channel_id=1, source_target_pairs={{0,8},{4,12},{8,0},{12,4},{1,9},{5,13},{9,1},{13,5},{2,10},{6,14},... | collective-permute-start | bytes 1769480 | tf_op jit(solution)/shard_map/ppermute | solution.py:21
  (218 other events, 2095.6 us)
Sparse Core Ops, SparseCore 0:
  572.9 137.3 all-reduce.3
